TPU v7x, 128 devices: a whole 4x4x4 slice. The times are simulated.
128 devices in a mesh: dp: 4 (over z_hi, core), expert: 32 (over z_lo, y, x).
Axes of the slice: x: 4, y: 4, z: 4 (z_hi: 2, z_lo: 2; z = z_hi * 2 + z_lo), core: 2. Of those that a mesh axis runs over, the one named last changes fastest.
Arguments:
- queries: bfloat16 [1024, 4096], P(('dp', 'expert')), may hold values from -9 to 9
- kv_pool: bfloat16 [16384, 16, 1024], P(('dp', 'expert')), may hold values from -9 to 9
- page_table: int32 [1024, 4, 16], P(('dp', 'expert')), may hold values from 0 to 127
- held_tokens: int32 [1024, 4], P(('dp', 'expert')), may hold values from 1 to 256, as said below
- sinks: float32 [64], replicated, may hold values from 2 to 8
- residual: bfloat16 [1024, 2880], P(('dp', 'expert')), may hold values from -100 to 100
- route_ids: int32 [1024, 4], P(('dp', 'expert')), may hold values from 0 to 31, all different within a row; in each aligned block of 8 rows (0 to 7, 8 to 15, ...) at most 2 rows name the same one
- route_weights: float32 [1024, 4], P(('dp', 'expert')), may hold values from 0.1 to 1
- moe_gain: float32 [2880], replicated, may hold values from 0.25 to 1.75
- w_gate: bfloat16 [32, 2880, 1536], P('expert', None, 'dp')
- w_up: bfloat16 [32, 2880, 1536], P('expert', None, 'dp')
- w_down: bfloat16 [32, 1536, 2880], P('expert', 'dp'), may hold values from -0.078125 to 0.078125
- o_weight: bfloat16 [4096, 2880], P(None, 'dp'), may hold values from -0.09375 to 0.09375
- attn_gain: float32 [2880], replicated, may hold values from 0.25 to 1.75
- qkv_weight: bfloat16 [2880, 5120], P(None, 'dp'), may hold values from -0.109375 to 0.109375
Outputs:
- next_stream: bfloat16 [1024, 2880], P(('dp', 'expert'))
- next_qkv: bfloat16 [1024, 5120], P(('dp', 'expert'))
Inputs may be any that keep to these rules, and one draw needn't show every extreme that they name: `route_ids`: each row names 4 different experts; among the 8 rows of one device no expert is named more than 2 times, a bound that some block reaches. `page_table`: pages may be shared between requests. `held_tokens`: the largest value is reached in every draw.
All inputs are finite; a program needn't handle non-finite values.
Results may differ from a plain program's by a relative error of at most 0.0145.
Values may be sent and summed in bfloat16 or wider, within the bound.
A program may use at most 128 MiB of HBM per device.

v0:
```python
import math
import jax
import jax.numpy as jnp
from jax import lax
from jax.sharding import PartitionSpec as P

HEADS = 64
KVH = 8
HD = 64
TOP = 4
PAGE = 16
PPH = 16
EPSILON = 1e-05
LIMIT = 7.0


def rms_scale(values, gain):
    wide = values.astype(jnp.float32)
    scale = lax.rsqrt(jnp.mean(wide * wide, axis=-1, keepdims=True) + EPSILON)
    return (wide * scale * gain).astype(jnp.bfloat16)


def scale_heads(numerator, factor):
    return numerator * jnp.repeat(factor, HD, axis=1)


def head_tables():
    groups = HEADS // KVH
    columns = jnp.arange(KVH * HD, dtype=jnp.int32)
    head_group = jnp.arange(HEADS, dtype=jnp.int32) // groups
    head_mask = columns[None, :] // HD == head_group[:, None]
    fold_table = (columns[:, None] % HD == jnp.arange(HD, dtype=jnp.int32)[None, :]).astype(
        jnp.float32
    )
    return (head_mask, fold_table)


def holder_block(query_rows, page_rows, count_rows, kv_pool, head_mask, fold_table):
    blocks = query_rows.shape[0]
    token_span = PPH * PAGE
    width = KVH * HD
    fetched = kv_pool[page_rows].reshape(blocks, token_span, 2 * width)
    keys_part = fetched[:, :, :width]
    values_part = fetched[:, :, width:]
    query_heads = query_rows.reshape(blocks, HEADS, HD)
    spread = jnp.where(
        head_mask[None], jnp.tile(query_heads, (1, 1, KVH)), jnp.zeros((), jnp.bfloat16)
    )
    scores = jnp.einsum("bhe,ble->bhl", spread, keys_part, preferred_element_type=jnp.float32) * (
        1.0 / math.sqrt(HD)
    )
    usable = (jnp.arange(token_span, dtype=jnp.int32)[None, :] < count_rows[:, None])[:, None, :]
    highest = jnp.max(jnp.where(usable, scores, -1e30), axis=-1)
    weights = jnp.where(usable, jnp.exp(scores - highest[..., None]), 0.0)
    totals = jnp.sum(weights, axis=-1)
    every_value = jnp.einsum(
        "bhl,ble->bhe",
        weights.astype(jnp.bfloat16),
        values_part,
        preferred_element_type=jnp.float32,
    )
    own_value = jnp.where(head_mask[None], every_value, 0.0)
    numerator = jnp.einsum("bhe,ed->bhd", own_value, fold_table, precision=lax.Precision.HIGHEST)
    return (highest, totals, numerator.reshape(blocks, HEADS * HD))


def expert_apply(rows, gate_w, up_w, down_w):
    gate_proj = jnp.minimum(jnp.dot(rows, gate_w, preferred_element_type=jnp.float32), LIMIT)
    up_proj = jnp.clip(jnp.dot(rows, up_w, preferred_element_type=jnp.float32), -LIMIT, LIMIT)
    activated = (gate_proj * jax.nn.sigmoid(1.702 * gate_proj) * (up_proj + 1.0)).astype(
        jnp.bfloat16
    )
    return jnp.dot(activated, down_w, preferred_element_type=jnp.float32)


def body(
    queries,
    kv_pool,
    page_table,
    held_tokens,
    sinks,
    residual,
    route_ids,
    route_weights,
    moe_gain,
    w_gate,
    w_up,
    w_down,
    o_weight,
    attn_gain,
    qkv_weight,
):
    dp_count = lax.axis_size("dp")
    experts_count = lax.axis_size("expert")
    own_rows = queries.shape[0]
    tables, held_rows = (
        lax.all_gather(page_table, "dp", axis=0, tiled=True),
        lax.all_gather(held_tokens, "dp", axis=0, tiled=True),
    )
    group_queries = lax.all_gather(queries, "dp", axis=0, tiled=True)
    holder = lax.axis_index("dp")
    own_pages = lax.dynamic_index_in_dim(tables, holder, 1, keepdims=False)
    own_counts = lax.dynamic_index_in_dim(held_rows, holder, 1, keepdims=False)
    group_rows = group_queries.shape[0]
    block_rows = 32
    step_total = group_rows // block_rows
    head_mask, fold_table = head_tables()

    def run_block(items):
        return holder_block(items[0], items[1], items[2], kv_pool, head_mask, fold_table)

    highest, totals, numerator = lax.map(
        run_block,
        (
            group_queries.reshape(step_total, block_rows, HEADS * HD),
            own_pages.reshape(step_total, block_rows, PPH),
            own_counts.reshape(step_total, block_rows),
        ),
    )
    highest = highest.reshape(group_rows, HEADS)
    totals = totals.reshape(group_rows, HEADS)
    numerator = numerator.reshape(group_rows, HEADS * HD)
    peak_score = lax.pmax(highest, "dp")
    factor = jnp.exp(highest - peak_score)
    totals, numerator = (
        lax.psum((totals * factor).astype(jnp.bfloat16), "dp").astype(jnp.float32),
        lax.psum(scale_heads(numerator, factor).astype(jnp.bfloat16), "dp").astype(jnp.float32),
    )
    highest = peak_score
    ceiling = jnp.maximum(highest, sinks[None, :])
    kept = jnp.exp(highest - ceiling)
    denominator = totals * kept + jnp.exp(sinks[None, :] - ceiling)
    attention = scale_heads(numerator, kept / denominator).astype(jnp.bfloat16)
    projected = jnp.dot(attention, o_weight, preferred_element_type=jnp.float32).astype(
        jnp.bfloat16
    )
    attention_out = lax.all_to_all(projected, "dp", split_axis=0, concat_axis=1, tiled=True)
    stream = (residual.astype(jnp.float32) + attention_out.astype(jnp.float32)).astype(jnp.bfloat16)
    moe_input = rms_scale(stream, moe_gain)
    capacity = 2 * own_rows * TOP // experts_count
    chosen = (
        route_ids[:, :, None] == jnp.arange(experts_count, dtype=jnp.int32)[None, None, :]
    ).astype(jnp.int32)
    flat_chosen = chosen.reshape(own_rows * TOP, experts_count)
    before = jnp.cumsum(flat_chosen, axis=0) - flat_chosen
    slot_index = jnp.sum(before * flat_chosen, axis=1).reshape(own_rows, TOP)
    placed = chosen[:, :, :, None] * (
        slot_index[:, :, None, None] == jnp.arange(capacity, dtype=jnp.int32)[None, None, None, :]
    ).astype(jnp.int32)
    placed = placed.reshape(own_rows, TOP, experts_count * capacity)
    dispatch = jnp.sum(placed, axis=1).astype(jnp.bfloat16)
    route_share = route_weights / jnp.sum(route_weights, axis=1, keepdims=True)
    combine = jnp.einsum(
        "rk,rkc->rc", route_share, placed.astype(jnp.float32), precision=lax.Precision.HIGHEST
    )
    send_rows = jnp.einsum(
        "rc,rd->cd", dispatch, moe_input, preferred_element_type=jnp.float32
    ).astype(jnp.bfloat16)
    gate_local = w_gate[0]
    up_local = w_up[0]
    down_local = w_down[0]
    copies = jnp.broadcast_to(send_rows[None], (dp_count,) + send_rows.shape).reshape(
        dp_count * send_rows.shape[0], send_rows.shape[1]
    )
    arrived = lax.all_to_all(copies, ("dp", "expert"), split_axis=0, concat_axis=0, tiled=True)
    partial_value = expert_apply(arrived, gate_local, up_local, down_local)
    came_back = lax.all_to_all(
        partial_value.astype(jnp.bfloat16),
        ("dp", "expert"),
        split_axis=0,
        concat_axis=0,
        tiled=True,
    ).astype(partial_value.dtype)
    returned = jnp.sum(came_back.reshape(dp_count, send_rows.shape[0], send_rows.shape[1]), axis=0)
    moe_out = jnp.dot(
        combine, returned, precision=lax.Precision.HIGHEST, preferred_element_type=jnp.float32
    )
    next_stream = (stream.astype(jnp.float32) + moe_out).astype(jnp.bfloat16)
    qkv_input = rms_scale(next_stream, attn_gain)
    group_qkv = jnp.dot(
        lax.all_gather(qkv_input, "dp", axis=0, tiled=True),
        qkv_weight,
        preferred_element_type=jnp.float32,
    ).astype(jnp.bfloat16)
    next_qkv = lax.all_to_all(group_qkv, "dp", split_axis=0, concat_axis=1, tiled=True)
    return (next_stream, next_qkv)


def solution(mesh):
    in_specs = (
        P(("dp", "expert"), None),
        P(("dp", "expert"), None, None),
        P(("dp", "expert"), None, None),
        P(("dp", "expert"), None),
        P(),
        P(("dp", "expert"), None),
        P(("dp", "expert"), None),
        P(("dp", "expert"), None),
        P(),
        P("expert", None, "dp"),
        P("expert", None, "dp"),
        P("expert", "dp", None),
        P(None, "dp"),
        P(),
        P(None, "dp"),
    )
    out_specs = (P(("dp", "expert"), None), P(("dp", "expert"), None))
    return jax.shard_map(body, mesh=mesh, in_specs=in_specs, out_specs=out_specs, check_vma=False)
```

profile of v0, /device:TPU:1, one launch (start us, length us, event | category | flops | bytes accessed | tf_op | source)
XLA Modules:
  0.0 265.4 jit_solution(2009156426341383861)
XLA Ops:
  7.3 8.6 %all-gather = s32[4,8,4]{1,2,0:T(4,128)S(1)} all-gather(s32[1,8,4]{1,2,0:T(4,128)} %bitcast.60), channel_id=1, replica_groups=mesh['dp'=4,'expert'=32] {'dp'}, dimensions={0}, use_global_device_ids=true | all-gather | bytes 640 | tf_op jit(solution)/shard_map/all_gather | solution.py:98
  16.1 7.2 %all_gather.14 = s32[32,4,16]{2,1,0:T(4,128)S(1)} all-gather(s32[8,4,16]{2,1,0:T(4,128)} %param.17), channel_id=1, replica_groups=mesh['dp'=4,'expert'=32] {'dp'}, dimensions={0}, use_global_device_ids=true | all-gather | bytes 10240 | tf_op jit(solution)/shard_map/all_gather | solution.py:97
  23.4 7.7 %all_gather.13 = bf16[32,4096]{1,0:T(8,128)(2,1)S(1)} all-gather(bf16[8,4096]{1,0:T(8,128)(2,1)} %param.15), channel_id=1, replica_groups=mesh['dp'=4,'expert'=32] {'dp'}, dimensions={0}, use_global_device_ids=true | all-gather | bytes 327680 | tf_op jit(solution)/shard_map/all_gather | solution.py:100
  31.7 2.7 %tile.15 = bf16[32,64,8,64]{3,2,1,0:T(8,128)(2,1)} broadcast(bf16[32,64,64]{2,1,0:T(8,128)(2,1)S(1)} %tile.14), dimensions={0,1,3} | broadcast | bytes 2359296 | tf_op jit(solution)/shard_map/while/body/eval_jaxpr/tile | solution.py:47
  34.4 6.4 %tile.16 = bf16[32,64,512]{2,1,0:T(8,128)(2,1)} reshape(bf16[32,64,8,64]{3,2,1,0:T(8,128)(2,1)} %tile.15) | data formatting | bytes 4194304 | tf_op jit(solution)/shard_map/while/body/eval_jaxpr/tile | solution.py:47
  40.8 16.1 %gather_fusion = bf16[512,16,1024]{2,1,0:T(8,128)(2,1)} fusion(bf16[128,16,1024]{2,1,0:T(8,128)(2,1)} %param.16, s32[1024]{0:T(1024)S(1)} %pad_clamp_fusion), kind=kCustom, calls=%fused_computation | custom fusion | bytes 33556480 | tf_op jit(solution)/shard_map/while/body/eval_jaxpr/gather | solution.py:42
  57.0 8.0 %select_reduce_fusion = (f32[32,64]{1,0:T(8,128)S(1)}, f32[32,64,256]{2,1,0:T(8,128)}) fusion(pred[32,256]{1,0:T(8,128)(4,1)S(1)} %iota_compare_fusion.2, bf16[32,256,1024]{2,1,0:T(8,128)(2,1)} %bitcast.54, bf16[32,64,512]{2,1,0:T(8,128)(2,1)} %tile.16, pred[64,512]{1,0:T(8,128)(4,1)S(1)} %broadcast_compare_fusion), kind=kOutput, calls=%fused_computation.20 | convolution fusion | flops 539490304 | bytes 12632064 | tf_op jit(solution)/shard_map/while/body/eval_jaxpr/bhe,ble->bhl/dot_general | solution.py:49
  65.1 12.4 %pmax.7 = f32[32,64]{1,0:T(8,128)S(1)} all-reduce(f32[32,64]{1,0:T(8,128)S(1)} %get-tuple-element.28), channel_id=1, replica_groups=mesh['dp'=4,'expert'=32] {'dp'}, use_global_device_ids=true, to_apply=%region_1.2 | all-reduce | flops 2048 | bytes 16384 | tf_op jit(solution)/shard_map/pmax | solution.py:123
  77.5 2.5 fusion.17
  80.0 4.3 %fusion = f32[32,64,512]{2,1,0:T(8,128)S(1)} fusion(bf16[32,256,1024]{2,1,0:T(8,128)(2,1)} %bitcast.55, f32[32,64,256]{2,1,0:T(8,128)S(1)} %copy-done.1, f32[32,64]{1,0:T(8,128)S(1)} %get-tuple-element.28, pred[32,256]{1,0:T(8,128)(4,1)S(1)} %iota_compare_fusion.2), kind=kOutput, calls=%fused_computation.1 | convolution fusion | flops 538968064 | bytes 14696448 | tf_op jit(solution)/shard_map/while/body/eval_jaxpr/bhl,ble->bhe/dot_general | solution.py:56
  84.4 2.2 fusion.22
  86.6 1.2 convert_element_type.109
  87.8 10.5 %psum.15 = bf16[32,64]{1,0:T(8,128)(2,1)S(1)} all-reduce(bf16[32,64]{1,0:T(8,128)(2,1)S(1)} %get-tuple-element.24), channel_id=1, replica_groups=mesh['dp'=4,'expert'=32] {'dp'}, use_global_device_ids=true, to_apply=%region_4.5 | all-reduce | flops 2048 | bytes 8192 | tf_op jit(solution)/shard_map/psum | solution.py:126
  100.6 30.9 %all-reduce.2.cloned.1.call-done = bf16[32,4096]{1,0:T(8,128)(2,1)} async-done(((bf16[32,4096]{1,0:T(8,128)(2,1)}), bf16[32,4096]{1,0:T(8,128)(2,1)}) %all-reduce.2.cloned.1.call-update) | async-done | bytes 262160 | tf_op jit(solution)/shard_map/psum | solution.py:127
  131.5 5.3 %fusion.40 = bf16[4,8,720]{2,1,0:T(8,128)(2,1)} fusion(bf16[4096,720]{0,1:T(8,128)(2,1)} %param.27, f32[32,4096]{1,0:T(8,128)} %reshape.243, bf16[32,4096]{1,0:T(8,128)(2,1)} %all-reduce.2.cloned.1.call-done), kind=kOutput, calls=%fused_computation.34 | convolution fusion | flops 189159936 | bytes 6730752 | tf_op jit(solution)/shard_map/dot_general | solution.py:134
  136.9 3.4 %all-to-all-start = ((bf16[4,8,720]{2,1,0:T(8,128)(2,1)}), bf16[4,8,720]{2,1,0:T(8,128)(2,1)S(1)}, u32[]{:S(2)}, u32[]{:S(2)}) async-start(bf16[4,8,720]{2,1,0:T(8,128)(2,1)} %fusion.40), calls=%async_computation | async-start | bytes 98304 | tf_op jit(solution)/shard_map/all_to_all | solution.py:137
  140.4 4.6 %all-to-all-done = bf16[4,8,720]{2,1,0:T(8,128)(2,1)S(1)} async-done(((bf16[4,8,720]{2,1,0:T(8,128)(2,1)}), bf16[4,8,720]{2,1,0:T(8,128)(2,1)S(1)}, u32[]{:S(2)}, u32[]{:S(2)}) %all-to-all-start) | async-done | bytes 46112 | tf_op jit(solution)/shard_map/all_to_all | solution.py:137
  145.7 1.2 broadcast_in_dim.109
  146.9 4.3 %all_to_all.40 = bf16[128,2,2880]{2,1,0:T(2,128)(2,1)} reshape(bf16[4,64,2880]{2,1,0:T(8,128)(2,1)} %broadcast_in_dim.109) | data formatting | bytes 2949120 | tf_op jit(solution)/shard_map/all_to_all | solution.py:165
  151.2 30.7 %all_to_all.53 = bf16[128,2,2880]{2,1,0:T(2,128)(2,1)} all-to-all(bf16[128,2,2880]{2,1,0:T(2,128)(2,1)} %all_to_all.40), channel_id=1, replica_groups=mesh['dp'=4,'expert'=32] {'dp','expert'}, dimensions={0} | all-to-all | bytes 2949120 | tf_op jit(solution)/shard_map/all_to_all | solution.py:165
  181.9 4.4 %all_to_all.42 = bf16[256,2880]{1,0:T(8,128)(2,1)} reshape(bf16[128,2,2880]{2,1,0:T(2,128)(2,1)} %all_to_all.53) | data formatting | bytes 2949120 | tf_op jit(solution)/shard_map/all_to_all | solution.py:165
  186.3 3.0 %fusion.25 = f32[256,384]{1,0:T(8,128)S(1)} fusion(bf16[256,2880]{1,0:T(8,128)(2,1)} %all_to_all.42, bf16[1,2880,384]{2,1,0:T(8,128)(2,1)} %param.24), kind=kOutput, calls=%fused_computation.28 | convolution fusion | flops 566329344 | bytes 4079616 | tf_op jit(solution)/shard_map/dot_general | solution.py:68
  189.3 5.1 %convolution_convert_fusion = bf16[256,2880]{0,1:T(8,128)(2,1)} fusion(bf16[1,384,2880]{1,2,0:T(8,128)(2,1)S(1)} %copy-done, bf16[256,2880]{1,0:T(8,128)(2,1)} %all_to_all.42, bf16[1,2880,384]{2,1,0:T(8,128)(2,1)} %param.25, f32[256,384]{1,0:T(8,128)S(1)} %fusion.25), kind=kOutput, calls=%fused_computation.7 | convolution fusion | flops 1134084096 | bytes 7766016 | tf_op jit(solution)/shard_map/dot_general | solution.py:73
  194.4 2.6 copy.30
  197.0 4.3 %all_to_all.43 = bf16[128,2,2880]{2,1,0:T(2,128)(2,1)} reshape(bf16[256,2880]{1,0:T(8,128)(2,1)} %copy.30) | data formatting | bytes 2949120 | tf_op jit(solution)/shard_map/all_to_all | solution.py:167
  201.3 6.1 %all-to-all-start.2 = ((bf16[128,2,2880]{2,1,0:T(2,128)(2,1)}), bf16[128,2,2880]{2,1,0:T(2,128)(2,1)}, u32[]{:S(2)}, u32[]{:S(2)}) async-start(bf16[128,2,2880]{2,1,0:T(2,128)(2,1)} %all_to_all.43), calls=%async_computation.2 | async-start | bytes 3014656 | tf_op jit(solution)/shard_map/all_to_all | solution.py:167
  207.4 23.1 %all-to-all-done.2 = bf16[128,2,2880]{2,1,0:T(2,128)(2,1)} async-done(((bf16[128,2,2880]{2,1,0:T(2,128)(2,1)}), bf16[128,2,2880]{2,1,0:T(2,128)(2,1)}, u32[]{:S(2)}, u32[]{:S(2)}) %all-to-all-start.2) | async-done | bytes 1474592 | tf_op jit(solution)/shard_map/all_to_all | solution.py:167
  230.5 4.5 %reshape.245 = f32[4,64,2880]{2,1,0:T(8,128)} reshape(bf16[128,2,2880]{2,1,0:T(2,128)(2,1)} %all-to-all-done.2) | data formatting | bytes 4423680 | tf_op jit(solution)/shard_map/convert_element_type | solution.py:173
  235.1 2.1 reduce_sum.69
  237.9 8.4 %all_gather.15 = bf16[32,2880]{1,0:T(8,128)(2,1)S(1)} all-gather(bf16[8,2880]{1,0:T(8,128)(2,1)S(1)} %fusion.63), channel_id=1, replica_groups=mesh['dp'=4,'expert'=32] {'dp'}, dimensions={0}, use_global_device_ids=true | all-gather | bytes 230400 | tf_op jit(solution)/shard_map/all_gather | solution.py:181
  246.3 4.3 %fusion.7 = bf16[4,8,1280]{2,1,0:T(8,128)(2,1)S(1)} fusion(bf16[32,2880]{1,0:T(8,128)(2,1)S(1)} %all_gather.15, bf16[2880,1280]{1,0:T(8,128)(2,1)} %param.29), kind=kOutput, calls=%fused_computation.12 | convolution fusion | flops 235970560 | bytes 7639040 | tf_op jit(solution)/shard_map/dot_general | solution.py:180
  250.6 7.3 %all_to_all.54 = bf16[4,8,1280]{2,1,0:T(8,128)(2,1)S(1)} all-to-all(bf16[4,8,1280]{2,1,0:T(8,128)(2,1)S(1)} %fusion.7), channel_id=1, replica_groups=mesh['dp'=4,'expert'=32] {'dp'}, dimensions={0} | all-to-all | bytes 163840 | tf_op jit(solution)/shard_map/all_to_all | solution.py:185
  (61 shorter events, 5.3 us)
Async XLA Ops:
  7.2 182.2 %copy-start = (bf16[1,384,2880]{1,2,0:T(8,128)(2,1)S(1)}, bf16[1,384,2880]{1,2,0:T(8,128)(2,1)}, u32[]{:S(2)}) copy-start(bf16[1,384,2880]{1,2,0:T(8,128)(2,1)} %param.26) | copy-start | bytes 6635524
  7.2 124.3 %all-reduce.2.cloned.1.call-start = ((), (), s32[]{:S(2)}) async-start(), calls=%async_computation.4 | async-start | bytes 524288 | tf_op jit(solution)/shard_map/psum | solution.py:127
  77.5 2.5 copy-start.1
  84.4 14.0 %copy-start.6 = (s32[8,4]{0,1:T(4,128)S(1)}, s32[8,4]{0,1:T(4,128)}, u32[]{:S(2)}) copy-start(s32[8,4]{0,1:T(4,128)} %param.21) | copy-start | bytes 388
  84.4 14.6 %copy-start.8 = (f32[64]{0:T(128)S(1)}, f32[64]{0:T(128)}, u32[]{:S(2)}) copy-start(f32[64]{0:T(128)} %param.19) | copy-start | bytes 772
  100.6 44.6 %copy-start.3 = (bf16[8,2880]{1,0:T(8,128)(2,1)S(1)}, bf16[8,2880]{1,0:T(8,128)(2,1)}, u32[]{:S(2)}) copy-start(bf16[8,2880]{1,0:T(8,128)(2,1)} %param.20) | copy-start | bytes 138244
  100.6 44.8 %copy-start.5 = (f32[2880]{0:T(1024)S(1)}, f32[2880]{0:T(1024)}, u32[]{:S(2)}) copy-start(f32[2880]{0:T(1024)} %param.23) | copy-start | bytes 34564
  136.9 8.1 %all-to-all-start = ((bf16[4,8,720]{2,1,0:T(8,128)(2,1)}), bf16[4,8,720]{2,1,0:T(8,128)(2,1)S(1)}, u32[]{:S(2)}, u32[]{:S(2)}) async-start(bf16[4,8,720]{2,1,0:T(8,128)(2,1)} %fusion.40), calls=%async_computation | async-start | bytes 98304 | tf_op jit(solution)/shard_map/all_to_all | solution.py:137
  201.3 6.1 %copy-start.7 = (f32[8,4]{0,1:T(4,128)S(1)}, f32[8,4]{0,1:T(4,128)}, u32[]{:S(2)}) copy-start(f32[8,4]{0,1:T(4,128)} %param.22) | copy-start | bytes 388
  201.3 29.3 %all-to-all-start.2 = ((bf16[128,2,2880]{2,1,0:T(2,128)(2,1)}), bf16[128,2,2880]{2,1,0:T(2,128)(2,1)}, u32[]{:S(2)}, u32[]{:S(2)}) async-start(bf16[128,2,2880]{2,1,0:T(2,128)(2,1)} %all_to_all.43), calls=%async_computation.2 | async-start | bytes 3014656 | tf_op jit(solution)/shard_map/all_to_all | solution.py:167
  235.0 2.7 %copy-start.4 = (f32[2880]{0:T(1024)S(1)}, f32[2880]{0:T(1024)}, u32[]{:S(2)}) copy-start(f32[2880]{0:T(1024)} %param.28) | copy-start | bytes 34564
  237.8 12.8 %copy-start.2 = (bf16[8,2880]{1,0:T(8,128)(2,1)}, bf16[8,2880]{1,0:T(8,128)(2,1)S(1)}, u32[]{:S(2)}) copy-start(bf16[8,2880]{1,0:T(8,128)(2,1)S(1)} %get-tuple-element.44) | copy-start | bytes 138244
Sparse Core Ops, SparseCore 0:
  87.9 43.5 all-reduce.1
where the time goes:
time: 266 us; the launch traced here: 265 us
  blocking collectives  93 us (35%)
  waiting for transfers between devices  58.7 us (22%)
  local copies, waits for them, and re-layouts  51.1 us (19%)
  matrix products  33.2 us (12%)
  between operations  14.3 us (5%)
  starting transfers between devices  9.51 us (4%)
  other arithmetic  5.52 us (2%)
    psum x1, waiting for transfers between devices, body(): lax.psum(scale_heads(numerator, factor).astype(jnp.bfloat16), 'dp')  30.9 us
    all_to_all x1, blocking collectives, body(): lax.all_to_all(copies, ('dp', 'expert'), split_axis=0, concat_axis=0, til...  30.7 us
    all_to_all x1, waiting for transfers between devices, body(): lax.all_to_all(partial_value.astype(jnp.bfloat16), ('dp', 'expert'), spli...  23.1 us
    gather x1, local copies, waits for them, and re-layouts, holder_block(): fetched = kv_pool[page_rows].reshape(blocks, token_span, 2 * width)  16.1 us
    pmax x1, blocking collectives, body(): peak_score = lax.pmax(highest, 'dp')  12.4 us
    psum x1, blocking collectives, body(): lax.psum((totals * factor).astype(jnp.bfloat16), 'dp').astype(jnp.float32)  10.5 us
    another operation x3, local copies, waits for them, and re-layouts, holder_block(): jnp.tile(query_heads, (1, 1, KVH))  9.71 us
    all_to_all x2, local copies, waits for them, and re-layouts, body(): lax.all_to_all(copies, ('dp', 'expert'), split_axis=0, concat_axis=0, til...  8.73 us
  transfers between devices with their start and end apart: 3, of which 3 were waited for; matrix products, arithmetic and copies ran while one was open for 1% of the time, Pallas kernels for 0%

commit v1 on v0

--- a/solution.py
+++ b/solution.py
@@ -94,7 +94,9 @@
     experts_count = lax.axis_size("expert")
     own_rows = queries.shape[0]
     tables, held_rows = (
-        lax.all_gather(page_table, "dp", axis=0, tiled=True),
+        jnp.concatenate(
+            lax.all_to_all(jnp.stack([page_table] * lax.axis_size("dp")), "dp", 0, 0), axis=0
+        ),
         lax.all_gather(held_tokens, "dp", axis=0, tiled=True),
     )
     group_queries = lax.all_gather(queries, "dp", axis=0, tiled=True)

time: 266 us -> 269 us (1.011)
  blocking collectives: 93 us -> 84 us
  starting transfers between devices: 9.51 us -> 16.1 us
  local copies, waits for them, and re-layouts: 51.1 us -> 54 us
    all_gather x1 -> x0, blocking collectives: 7.2 us -> none  [body(): lax.all_gather(page_table, 'dp', axis=0, tiled=True)]
    all_to_all x0 -> x1, starting transfers between devices: none -> 6.65 us  [body(): lax.all_to_all(jnp.stack([page_table] * lax.axis_size('dp')), 'dp', 0, 0)]
  transfers between devices with their start and end apart: 3 -> 4, of which waited for: 3 -> 3; matrix products, arithmetic and copies ran while one was open for 1% -> 5% of each run, Pallas kernels for 0% -> 0%
where the time goes in v1:
time: 269 us; the launch traced here: 268 us
  blocking collectives  84 us (31%)
  waiting for transfers between devices  59.3 us (22%)
  local copies, waits for them, and re-layouts  54 us (20%)
  matrix products  33.2 us (12%)
  starting transfers between devices  16.1 us (6%)
  between operations  14.3 us (5%)
  other arithmetic  6.88 us (3%)
    psum x1, waiting for transfers between devices, body(): lax.psum(scale_heads(numerator, factor).astype(jnp.bfloat16), 'dp')  31.6 us
    all_to_all x1, blocking collectives, body(): lax.all_to_all(copies, ('dp', 'expert'), split_axis=0, concat_axis=0, til...  30.7 us
    all_to_all x1, waiting for transfers between devices, body(): lax.all_to_all(partial_value.astype(jnp.bfloat16), ('dp', 'expert'), spli...  23.1 us
    gather x1, local copies, waits for them, and re-layouts, holder_block(): fetched = kv_pool[page_rows].reshape(blocks, token_span, 2 * width)  16.1 us
    pmax x1, blocking collectives, body(): peak_score = lax.pmax(highest, 'dp')  12.4 us
    psum x1, blocking collectives, body(): lax.psum((totals * factor).astype(jnp.bfloat16), 'dp').astype(jnp.float32)  10.5 us
    another operation x3, local copies, waits for them, and re-layouts, holder_block(): jnp.tile(query_heads, (1, 1, KVH))  9.71 us
    all_to_all x2, local copies, waits for them, and re-layouts, body(): lax.all_to_all(copies, ('dp', 'expert'), split_axis=0, concat_axis=0, til...  8.73 us
  transfers between devices with their start and end apart: 4, of which 3 were waited for; matrix products, arithmetic and copies ran while one was open for 5% of the time, Pallas kernels for 0%

profile of v1, /device:TPU:1, one launch (start us, length us, event | category | flops | bytes accessed | tf_op | source)
XLA Modules:
  0.0 267.8 jit_solution(2783574315657916639)
XLA Ops:
  8.8 6.6 %all-to-all-start = ((s32[4,1,512]{2,1,0:T(1,128)}), s32[4,1,512]{2,1,0:T(1,128)S(1)}, u32[]{:S(2)}, u32[]{:S(2)}) async-start(s32[4,1,512]{2,1,0:T(1,128)} %reshape.267), calls=%async_computation | async-start | bytes 16384 | tf_op jit(solution)/shard_map/all_to_all | solution.py:98
  16.9 6.7 %all-gather = s32[4,8,4]{1,2,0:T(4,128)S(1)} all-gather(s32[1,8,4]{1,2,0:T(4,128)} %bitcast.67), channel_id=1, replica_groups=mesh['dp'=4,'expert'=32] {'dp'}, dimensions={0}, use_global_device_ids=true | all-gather | bytes 640 | tf_op jit(solution)/shard_map/all_gather | solution.py:100
  24.2 7.9 %all_gather.10 = bf16[32,4096]{1,0:T(8,128)(2,1)S(1)} all-gather(bf16[8,4096]{1,0:T(8,128)(2,1)} %param.15), channel_id=1, replica_groups=mesh['dp'=4,'expert'=32] {'dp'}, dimensions={0}, use_global_device_ids=true | all-gather | bytes 327680 | tf_op jit(solution)/shard_map/all_gather | solution.py:102
  32.7 2.7 %tile.15 = bf16[32,64,8,64]{3,2,1,0:T(8,128)(2,1)} broadcast(bf16[32,64,64]{2,1,0:T(8,128)(2,1)S(1)} %tile.14), dimensions={0,1,3} | broadcast | bytes 2359296 | tf_op jit(solution)/shard_map/while/body/eval_jaxpr/tile | solution.py:47
  35.4 6.4 %tile.16 = bf16[32,64,512]{2,1,0:T(8,128)(2,1)} reshape(bf16[32,64,8,64]{3,2,1,0:T(8,128)(2,1)} %tile.15) | data formatting | bytes 4194304 | tf_op jit(solution)/shard_map/while/body/eval_jaxpr/tile | solution.py:47
  43.5 16.1 %gather_fusion = bf16[512,16,1024]{2,1,0:T(8,128)(2,1)} fusion(bf16[128,16,1024]{2,1,0:T(8,128)(2,1)} %param.16, s32[1024]{0:T(1024)S(1)} %pad_clamp_fusion), kind=kCustom, calls=%fused_computation | custom fusion | bytes 33556480 | tf_op jit(solution)/shard_map/while/body/eval_jaxpr/gather | solution.py:42
  59.5 8.0 %select_reduce_fusion = (f32[32,64]{1,0:T(8,128)S(1)}, f32[32,64,256]{2,1,0:T(8,128)}) fusion(pred[32,256]{1,0:T(8,128)(4,1)S(1)} %iota_compare_fusion.2, bf16[32,256,1024]{2,1,0:T(8,128)(2,1)} %bitcast.62, bf16[32,64,512]{2,1,0:T(8,128)(2,1)} %tile.16, pred[64,512]{1,0:T(8,128)(4,1)S(1)} %broadcast_compare_fusion), kind=kOutput, calls=%fused_computation.20 | convolution fusion | flops 539490304 | bytes 12632064 | tf_op jit(solution)/shard_map/while/body/eval_jaxpr/bhe,ble->bhl/dot_general | solution.py:49
  67.6 12.4 %pmax.7 = f32[32,64]{1,0:T(8,128)S(1)} all-reduce(f32[32,64]{1,0:T(8,128)S(1)} %get-tuple-element.28), channel_id=1, replica_groups=mesh['dp'=4,'expert'=32] {'dp'}, use_global_device_ids=true, to_apply=%region_1.2 | all-reduce | flops 2048 | bytes 16384 | tf_op jit(solution)/shard_map/pmax | solution.py:125
  80.0 2.5 fusion.17
  82.5 4.3 %fusion = f32[32,64,512]{2,1,0:T(8,128)S(1)} fusion(bf16[32,256,1024]{2,1,0:T(8,128)(2,1)} %bitcast.63, f32[32,64,256]{2,1,0:T(8,128)S(1)} %copy-done.1, f32[32,64]{1,0:T(8,128)S(1)} %get-tuple-element.28, pred[32,256]{1,0:T(8,128)(4,1)S(1)} %iota_compare_fusion.2), kind=kOutput, calls=%fused_computation.1 | convolution fusion | flops 538968064 | bytes 14696448 | tf_op jit(solution)/shard_map/while/body/eval_jaxpr/bhl,ble->bhe/dot_general | solution.py:56
  86.9 2.2 fusion.22
  89.1 1.2 convert_element_type.109
  90.3 10.5 %psum.15 = bf16[32,64]{1,0:T(8,128)(2,1)S(1)} all-reduce(bf16[32,64]{1,0:T(8,128)(2,1)S(1)} %get-tuple-element.24), channel_id=1, replica_groups=mesh['dp'=4,'expert'=32] {'dp'}, use_global_device_ids=true, to_apply=%region_4.5 | all-reduce | flops 2048 | bytes 8192 | tf_op jit(solution)/shard_map/psum | solution.py:128
  102.4 31.6 %all-reduce.2.cloned.1.call-done = bf16[32,4096]{1,0:T(8,128)(2,1)} async-done(((bf16[32,4096]{1,0:T(8,128)(2,1)}), bf16[32,4096]{1,0:T(8,128)(2,1)}) %all-reduce.2.cloned.1.call-update) | async-done | bytes 262160 | tf_op jit(solution)/shard_map/psum | solution.py:129
  134.0 5.3 %fusion.40 = bf16[4,8,720]{2,1,0:T(8,128)(2,1)} fusion(bf16[4096,720]{0,1:T(8,128)(2,1)} %param.27, f32[32,4096]{1,0:T(8,128)} %reshape.249, bf16[32,4096]{1,0:T(8,128)(2,1)} %all-reduce.2.cloned.1.call-done), kind=kOutput, calls=%fused_computation.34 | convolution fusion | flops 189159936 | bytes 6730752 | tf_op jit(solution)/shard_map/dot_general | solution.py:136
  139.3 3.4 %all-to-all-start.1 = ((bf16[4,8,720]{2,1,0:T(8,128)(2,1)}), bf16[4,8,720]{2,1,0:T(8,128)(2,1)S(1)}, u32[]{:S(2)}, u32[]{:S(2)}) async-start(bf16[4,8,720]{2,1,0:T(8,128)(2,1)} %fusion.40), calls=%async_computation.1 | async-start | bytes 98304 | tf_op jit(solution)/shard_map/all_to_all | solution.py:139
  142.8 4.6 %all-to-all-done.1 = bf16[4,8,720]{2,1,0:T(8,128)(2,1)S(1)} async-done(((bf16[4,8,720]{2,1,0:T(8,128)(2,1)}), bf16[4,8,720]{2,1,0:T(8,128)(2,1)S(1)}, u32[]{:S(2)}, u32[]{:S(2)}) %all-to-all-start.1) | async-done | bytes 46112 | tf_op jit(solution)/shard_map/all_to_all | solution.py:139
  148.1 1.2 broadcast_in_dim.109
  149.3 4.3 %all_to_all.44 = bf16[128,2,2880]{2,1,0:T(2,128)(2,1)} reshape(bf16[4,64,2880]{2,1,0:T(8,128)(2,1)} %broadcast_in_dim.109) | data formatting | bytes 2949120 | tf_op jit(solution)/shard_map/all_to_all | solution.py:167
  153.6 30.7 %all_to_all.58 = bf16[128,2,2880]{2,1,0:T(2,128)(2,1)} all-to-all(bf16[128,2,2880]{2,1,0:T(2,128)(2,1)} %all_to_all.44), channel_id=1, replica_groups=mesh['dp'=4,'expert'=32] {'dp','expert'}, dimensions={0} | all-to-all | bytes 2949120 | tf_op jit(solution)/shard_map/all_to_all | solution.py:167
  184.3 4.4 %all_to_all.46 = bf16[256,2880]{1,0:T(8,128)(2,1)} reshape(bf16[128,2,2880]{2,1,0:T(2,128)(2,1)} %all_to_all.58) | data formatting | bytes 2949120 | tf_op jit(solution)/shard_map/all_to_all | solution.py:167
  188.7 3.0 %fusion.25 = f32[256,384]{1,0:T(8,128)S(1)} fusion(bf16[256,2880]{1,0:T(8,128)(2,1)} %all_to_all.46, bf16[1,2880,384]{2,1,0:T(8,128)(2,1)} %param.24), kind=kOutput, calls=%fused_computation.28 | convolution fusion | flops 566329344 | bytes 4079616 | tf_op jit(solution)/shard_map/dot_general | solution.py:68
  191.8 5.1 %convolution_convert_fusion = bf16[256,2880]{0,1:T(8,128)(2,1)} fusion(bf16[1,384,2880]{1,2,0:T(8,128)(2,1)S(1)} %copy-done, bf16[256,2880]{1,0:T(8,128)(2,1)} %all_to_all.46, bf16[1,2880,384]{2,1,0:T(8,128)(2,1)} %param.25, f32[256,384]{1,0:T(8,128)S(1)} %fusion.25), kind=kOutput, calls=%fused_computation.7 | convolution fusion | flops 1134084096 | bytes 7766016 | tf_op jit(solution)/shard_map/dot_general | solution.py:73
  196.8 2.6 copy.39
  199.4 4.3 %all_to_all.47 = bf16[128,2,2880]{2,1,0:T(2,128)(2,1)} reshape(bf16[256,2880]{1,0:T(8,128)(2,1)} %copy.39) | data formatting | bytes 2949120 | tf_op jit(solution)/shard_map/all_to_all | solution.py:169
  203.7 6.1 %all-to-all-start.3 = ((bf16[128,2,2880]{2,1,0:T(2,128)(2,1)}), bf16[128,2,2880]{2,1,0:T(2,128)(2,1)}, u32[]{:S(2)}, u32[]{:S(2)}) async-start(bf16[128,2,2880]{2,1,0:T(2,128)(2,1)} %all_to_all.47), calls=%async_computation.3 | async-start | bytes 3014656 | tf_op jit(solution)/shard_map/all_to_all | solution.py:169
  209.8 23.1 %all-to-all-done.3 = bf16[128,2,2880]{2,1,0:T(2,128)(2,1)} async-done(((bf16[128,2,2880]{2,1,0:T(2,128)(2,1)}), bf16[128,2,2880]{2,1,0:T(2,128)(2,1)}, u32[]{:S(2)}, u32[]{:S(2)}) %all-to-all-start.3) | async-done | bytes 1474592 | tf_op jit(solution)/shard_map/all_to_all | solution.py:169
  233.0 4.5 %reshape.251 = f32[4,64,2880]{2,1,0:T(8,128)} reshape(bf16[128,2,2880]{2,1,0:T(2,128)(2,1)} %all-to-all-done.3) | data formatting | bytes 4423680 | tf_op jit(solution)/shard_map/convert_element_type | solution.py:175
  237.5 2.1 reduce_sum.69
  240.3 8.4 %all_gather.11 = bf16[32,2880]{1,0:T(8,128)(2,1)S(1)} all-gather(bf16[8,2880]{1,0:T(8,128)(2,1)S(1)} %fusion.63), channel_id=1, replica_groups=mesh['dp'=4,'expert'=32] {'dp'}, dimensions={0}, use_global_device_ids=true | all-gather | bytes 230400 | tf_op jit(solution)/shard_map/all_gather | solution.py:183
  248.7 4.3 %fusion.7 = bf16[4,8,1280]{2,1,0:T(8,128)(2,1)S(1)} fusion(bf16[32,2880]{1,0:T(8,128)(2,1)S(1)} %all_gather.11, bf16[2880,1280]{1,0:T(8,128)(2,1)} %param.29), kind=kOutput, calls=%fused_computation.12 | convolution fusion | flops 235970560 | bytes 7639040 | tf_op jit(solution)/shard_map/dot_general | solution.py:182
  253.0 7.3 %all_to_all.59 = bf16[4,8,1280]{2,1,0:T(8,128)(2,1)S(1)} all-to-all(bf16[4,8,1280]{2,1,0:T(8,128)(2,1)S(1)} %fusion.7), channel_id=1, replica_groups=mesh['dp'=4,'expert'=32] {'dp'}, dimensions={0} | all-to-all | bytes 163840 | tf_op jit(solution)/shard_map/all_to_all | solution.py:187
  (66 shorter events, 9.4 us)
Async XLA Ops:
  7.2 184.6 %copy-start = (bf16[1,384,2880]{1,2,0:T(8,128)(2,1)S(1)}, bf16[1,384,2880]{1,2,0:T(8,128)(2,1)}, u32[]{:S(2)}) copy-start(bf16[1,384,2880]{1,2,0:T(8,128)(2,1)} %param.26) | copy-start | bytes 6635524
  8.8 33.3 %all-to-all-start = ((s32[4,1,512]{2,1,0:T(1,128)}), s32[4,1,512]{2,1,0:T(1,128)S(1)}, u32[]{:S(2)}, u32[]{:S(2)}) async-start(s32[4,1,512]{2,1,0:T(1,128)} %reshape.267), calls=%async_computation | async-start | bytes 16384 | tf_op jit(solution)/shard_map/all_to_all | solution.py:98
  15.4 118.6 %all-reduce.2.cloned.1.call-start = ((), (), s32[]{:S(2)}) async-start(), calls=%async_computation.5 | async-start | bytes 524288 | tf_op jit(solution)/shard_map/psum | solution.py:129
  80.0 2.5 copy-start.1
  86.9 14.0 %copy-start.7 = (f32[64]{0:T(128)S(1)}, f32[64]{0:T(128)}, u32[]{:S(2)}) copy-start(f32[64]{0:T(128)} %param.19) | copy-start | bytes 772
  102.4 45.3 %copy-start.3 = (bf16[8,2880]{1,0:T(8,128)(2,1)S(1)}, bf16[8,2880]{1,0:T(8,128)(2,1)}, u32[]{:S(2)}) copy-start(bf16[8,2880]{1,0:T(8,128)(2,1)} %param.20) | copy-start | bytes 138244
  102.4 45.4 %copy-start.5 = (f32[2880]{0:T(1024)S(1)}, f32[2880]{0:T(1024)}, u32[]{:S(2)}) copy-start(f32[2880]{0:T(1024)} %param.23) | copy-start | bytes 34564
  139.3 8.1 %all-to-all-start.1 = ((bf16[4,8,720]{2,1,0:T(8,128)(2,1)}), bf16[4,8,720]{2,1,0:T(8,128)(2,1)S(1)}, u32[]{:S(2)}, u32[]{:S(2)}) async-start(bf16[4,8,720]{2,1,0:T(8,128)(2,1)} %fusion.40), calls=%async_computation.1 | async-start | bytes 98304 | tf_op jit(solution)/shard_map/all_to_all | solution.py:139
  203.7 6.1 %copy-start.6 = (f32[8,4]{0,1:T(4,128)S(1)}, f32[8,4]{0,1:T(4,128)}, u32[]{:S(2)}) copy-start(f32[8,4]{0,1:T(4,128)} %param.22) | copy-start | bytes 388
  203.7 29.3 %all-to-all-start.3 = ((bf16[128,2,2880]{2,1,0:T(2,128)(2,1)}), bf16[128,2,2880]{2,1,0:T(2,128)(2,1)}, u32[]{:S(2)}, u32[]{:S(2)}) async-start(bf16[128,2,2880]{2,1,0:T(2,128)(2,1)} %all_to_all.47), calls=%async_computation.3 | async-start | bytes 3014656 | tf_op jit(solution)/shard_map/all_to_all | solution.py:169
  237.5 2.7 %copy-start.4 = (f32[2880]{0:T(1024)S(1)}, f32[2880]{0:T(1024)}, u32[]{:S(2)}) copy-start(f32[2880]{0:T(1024)} %param.28) | copy-start | bytes 34564
  240.2 12.8 %copy-start.2 = (bf16[8,2880]{1,0:T(8,128)(2,1)}, bf16[8,2880]{1,0:T(8,128)(2,1)S(1)}, u32[]{:S(2)}) copy-start(bf16[8,2880]{1,0:T(8,128)(2,1)S(1)} %get-tuple-element.44) | copy-start | bytes 138244
Sparse Core Ops, SparseCore 0:
  90.4 43.4 all-reduce.1
